TPU v7x, 32 devices: a whole 2x2x4 slice. The times are simulated.
32 devices in a mesh: row: 8 (over y, x, core), col: 4 (over z).
Axes of the slice: x: 2, y: 2, z: 4, core: 2. Of those that a mesh axis runs over, the one named last changes fastest.
Arguments:
- transitions: bfloat16 [4, 1024, 32768], P(None, 'row', 'col'), may hold values from 1.5199184e-06 to 0.00015258789
- values: bfloat16 [32768, 6144], P('row', 'col'), may hold values from -1280 to 1280
- earlier_sum: bfloat16 [4, 1024, 6144], P(None, 'row', 'col'), may hold values from -8 to 8
- section_costs: bfloat16 [4, 1024, 6144], P(None, 'row', 'col'), may hold values from 0 to 3
Outputs:
- backed_up: float32 [1024, 6144], P('row', 'col')
All inputs are finite; a program needn't handle non-finite values.
Results may differ from a plain program's by a relative error of at most 0.0003.
Values may be sent and summed in bfloat16 or wider, within the bound.
A program may use at most 192 MiB of HBM per device.

v0:
```python
import jax
import jax.numpy as jnp
from jax import lax
from jax.sharding import PartitionSpec as P

STEPS = 4


DISCOUNT = 0.97


def broadcast(value, axis, source):
    kept = jnp.where(lax.axis_index(axis) == source, value, 0).astype(value.dtype)
    return lax.psum(kept, axis)


def passed_along(value, axis, by):
    peers = lax.axis_size(axis)
    return lax.ppermute(value, axis, [(i, (i + by) % peers) for i in range(peers)])


def local(transitions, values, earlier_sum, section_costs):
    row_count = lax.axis_size("row")
    col_count = lax.axis_size("col")
    group_ratio = row_count // col_count
    row_index = lax.axis_index("row")
    block_width = values.shape[0]
    actions = transitions.shape[0]
    local_rows = transitions.shape[1]
    accumulated = earlier_sum.astype(jnp.float32)
    current = values
    for section in range(STEPS):
        column_block = (row_index + section) % row_count
        offered = lax.dynamic_slice_in_dim(
            transitions, column_block % group_ratio * block_width, block_width, 2
        )
        received = broadcast(offered, "col", column_block // group_ratio)
        product = jnp.dot(
            received.reshape(actions * local_rows, block_width),
            current,
            preferred_element_type=jnp.float32,
        )
        accumulated = accumulated + product.reshape(accumulated.shape)
        if section + 1 < STEPS:
            current = passed_along(current, "row", -1)
    return jnp.min(section_costs.astype(jnp.float32) + DISCOUNT * accumulated, axis=0)


def solution(mesh):
    in_specs = (
        P(None, "row", "col"),
        P("row", "col"),
        P(None, "row", "col"),
        P(None, "row", "col"),
    )
    out_specs = P("row", "col")
    return jax.shard_map(local, mesh=mesh, in_specs=in_specs, out_specs=out_specs, check_vma=False)
```

profile of v0, /device:TPU:25, one launch (start us, length us, event | category | flops | bytes accessed | tf_op | source)
XLA Modules:
  0.0 765.3 jit_solution(14365431897409120742)
XLA Ops:
  6.5 0.0 all-reduce.3.cloned.1.call-start
  6.5 0.7 collective-permute-start
  7.2 137.5 %collective-permute-done = bf16[4096,1536]{1,0:T(8,128)(2,1)} collective-permute-done((bf16[4096,1536]{1,0:T(8,128)(2,1)}, bf16[4096,1536]{1,0:T(8,128)(2,1)}, u32[]{:S(2)}, u32[]{:S(2)}) %collective-permute-start) | collective-permute-done | bytes 12582944 | tf_op jit(solution)/shard_map/ppermute | solution.py:19
  144.7 0.6 collective-permute-start.1
  145.3 11.5 %dynamic-slice_select_fusion = (bf16[4,128,4096]{2,1,0:T(8,128)(2,1)}, bf16[4,128,4096]{2,1,0:T(8,128)(2,1)}, bf16[4,128,4096]{2,1,0:T(8,128)(2,1)}, bf16[4,128,4096]{2,1,0:T(8,128)(2,1)}) fusion(bf16[4,128,8192]{2,1,0:T(8,128)(2,1)} %param.4, s32[]{:T(128)S(6)} %select_n.108, pred[]{:T(512)S(6)} %eq.24, s32[]{:T(128)S(6)} %select_n.96, pred[]{:T(512)S(6)} %eq.22, ...), kind=kLoop, calls=%fused_computation.8 | loop fusion | flops 8388608 | bytes 33554452 | tf_op jit(solution)/shard_map/jit(_where)/select_n | solution.py:13
  156.8 0.0 copy-start.3
  156.8 0.0 all-reduce.3.cloned.1.call-update
  156.8 126.3 %collective-permute-done.1 = bf16[4096,1536]{1,0:T(8,128)(2,1)} collective-permute-done((bf16[4096,1536]{1,0:T(8,128)(2,1)}, bf16[4096,1536]{1,0:T(8,128)(2,1)}, u32[]{:S(2)}, u32[]{:S(2)}) %collective-permute-start.1) | collective-permute-done | bytes 12582944 | tf_op jit(solution)/shard_map/ppermute | solution.py:19
  283.1 1.2 collective-permute-start.2
  284.4 433.6 %all-reduce.3.cloned.1.call-done = (bf16[4,128,4096]{2,1,0:T(8,128)(2,1)}, bf16[4,128,4096]{2,1,0:T(8,128)(2,1)}, bf16[4,128,4096]{2,1,0:T(8,128)(2,1)}, bf16[4,128,4096]{2,1,0:T(8,128)(2,1)}) async-done(((bf16[4,128,4096]{2,1,0:T(8,128)(2,1)}, bf16[4,128,4096]{2,1,0:T(8,128)(2,1)}, bf16[4,128,4096]{2,1,0:T(8,128)(2,1)}, bf16[4,128,4096]{2,1,0:T(8,128)(2,1)}), (bf16[4,128,4096]{2,1,0:T(8,128)(2,1)}, ...) | async-done | bytes 16777232 | tf_op jit(solution)/shard_map/psum | solution.py:14
  717.9 0.0 copy-done.3
  718.0 0.0 copy-start.2
  718.0 10.6 %fusion.8 = f32[4,128,1536]{2,1,0:T(8,128)S(1)} fusion(bf16[4,128,4096]{2,1,0:T(8,128)(2,1)} %get-tuple-element.5, bf16[4096,1536]{1,0:T(8,128)(2,1)} %param.5, bf16[4,128,1536]{2,1,0:T(8,128)(2,1)S(1)} %copy-done.3), kind=kOutput, calls=%fused_computation.12 | convolution fusion | flops 6444023808 | bytes 21495808 | tf_op jit(solution)/shard_map/dot_general | solution.py:38
  728.6 0.0 copy-done.2
  728.6 0.0 copy-start.1
  728.6 9.5 %fusion.11 = f32[4,128,1536]{2,1,0:T(8,128)S(1)} fusion(f32[4,128,1536]{2,1,0:T(8,128)S(1)} %fusion.8, bf16[4,128,4096]{2,1,0:T(8,128)(2,1)S(1)} %copy-done.2, bf16[4096,1536]{1,0:T(8,128)(2,1)} %collective-permute-done), kind=kOutput, calls=%fused_computation.13 | convolution fusion | flops 6443237376 | bytes 23068672 | tf_op jit(solution)/shard_map/dot_general | solution.py:38
  738.1 0.0 copy-done.1
  738.1 0.0 copy-start
  738.1 0.0 copy-start.4
  738.2 9.5 %fusion.14 = f32[4,128,1536]{2,1,0:T(8,128)S(1)} fusion(f32[4,128,1536]{2,1,0:T(8,128)S(1)} %fusion.11, bf16[4,128,4096]{2,1,0:T(8,128)(2,1)S(1)} %copy-done.1, bf16[4096,1536]{1,0:T(8,128)(2,1)} %collective-permute-done.1), kind=kOutput, calls=%fused_computation.14 | convolution fusion | flops 6443237376 | bytes 23068672 | tf_op jit(solution)/shard_map/dot_general | solution.py:38
  747.6 0.0 collective-permute-done.2
  747.6 0.0 copy-done
  747.7 0.0 copy-done.4
  747.7 10.8 %fusion.26 = f32[128,1536]{1,0:T(8,128)} fusion(f32[4,128,1536]{2,1,0:T(8,128)S(1)} %fusion.14, bf16[4,128,4096]{2,1,0:T(8,128)(2,1)S(1)} %copy-done, bf16[4096,1536]{1,0:T(8,128)(2,1)} %collective-permute-done.2, bf16[4,128,1536]{2,1,0:T(8,128)(2,1)S(1)} %copy-done.4), kind=kOutput, calls=%fused_computation.18 | convolution fusion | flops 6446186496 | bytes 22282240 | tf_op jit(solution)/shard_map/dot_general | solution.py:38
Async XLA Ops:
  6.5 711.4 %all-reduce.3.cloned.1.call-start = ((), (), s32[]{:S(2)}) async-start(), calls=%async_computation | async-start | bytes 33554432 | tf_op jit(solution)/shard_map/psum | solution.py:14
  6.5 138.2 %collective-permute-start = (bf16[4096,1536]{1,0:T(8,128)(2,1)}, bf16[4096,1536]{1,0:T(8,128)(2,1)}, u32[]{:S(2)}, u32[]{:S(2)}) collective-permute-start(bf16[4096,1536]{1,0:T(8,128)(2,1)} %param.5), channel_id=1, source_target_pairs={{0,28},{4,0},{8,4},{12,8},{16,12},{20,16},{24,20},{28,24},{1,29},{... | collective-permute-start | bytes 37748744 | tf_op jit(solution)/shard_map/ppermute | solution.py:19
  144.7 138.4 %collective-permute-start.1 = (bf16[4096,1536]{1,0:T(8,128)(2,1)}, bf16[4096,1536]{1,0:T(8,128)(2,1)}, u32[]{:S(2)}, u32[]{:S(2)}) collective-permute-start(bf16[4096,1536]{1,0:T(8,128)(2,1)} %collective-permute-done), channel_id=1, source_target_pairs={{0,28},{4,0},{8,4},{12,8},{16,12},{20,16},{24,20},{28,24},{1,29},{... | collective-permute-start | bytes 37748744 | tf_op jit(solution)/shard_map/ppermute | solution.py:19
  156.8 561.2 %copy-start.3 = (bf16[4,128,1536]{2,1,0:T(8,128)(2,1)S(1)}, bf16[4,128,1536]{2,1,0:T(8,128)(2,1)}, u32[]{:S(2)}) copy-start(bf16[4,128,1536]{2,1,0:T(8,128)(2,1)} %param.6) | copy-start | bytes 4718596
  283.1 464.5 %collective-permute-start.2 = (bf16[4096,1536]{1,0:T(8,128)(2,1)}, bf16[4096,1536]{1,0:T(8,128)(2,1)}, u32[]{:S(2)}, u32[]{:S(2)}) collective-permute-start(bf16[4096,1536]{1,0:T(8,128)(2,1)} %collective-permute-done.1), channel_id=1, source_target_pairs={{0,28},{4,0},{8,4},{12,8},{16,12},{20,16},{24,20},{28,24},{1,29},{... | collective-permute-start | bytes 37748744 | tf_op jit(solution)/shard_map/ppermute | solution.py:19
  718.0 10.7 %copy-start.2 = (bf16[4,128,4096]{2,1,0:T(8,128)(2,1)S(1)}, bf16[4,128,4096]{2,1,0:T(8,128)(2,1)}, u32[]{:S(2)}) copy-start(bf16[4,128,4096]{2,1,0:T(8,128)(2,1)} %get-tuple-element.6) | copy-start | bytes 12582916
  728.6 9.5 %copy-start.1 = (bf16[4,128,4096]{2,1,0:T(8,128)(2,1)S(1)}, bf16[4,128,4096]{2,1,0:T(8,128)(2,1)}, u32[]{:S(2)}) copy-start(bf16[4,128,4096]{2,1,0:T(8,128)(2,1)} %get-tuple-element.7) | copy-start | bytes 12582916
  738.1 9.5 %copy-start = (bf16[4,128,4096]{2,1,0:T(8,128)(2,1)S(1)}, bf16[4,128,4096]{2,1,0:T(8,128)(2,1)}, u32[]{:S(2)}) copy-start(bf16[4,128,4096]{2,1,0:T(8,128)(2,1)} %get-tuple-element.8) | copy-start | bytes 12582916
  738.1 9.5 %copy-start.4 = (bf16[4,128,1536]{2,1,0:T(8,128)(2,1)S(1)}, bf16[4,128,1536]{2,1,0:T(8,128)(2,1)}, u32[]{:S(2)}) copy-start(bf16[4,128,1536]{2,1,0:T(8,128)(2,1)} %param.7) | copy-start | bytes 4718596
Sparse Core Ops, SparseCore 0:
  156.9 560.9 all-reduce.2
where the time goes:
time: 770 us; the launch traced here: 765 us
  waiting for transfers between devices  697 us (91%)
  matrix products  40.4 us (5%)
  between operations  13.5 us (2%)
  other arithmetic  11.5 us (1%)
    psum x1, waiting for transfers between devices, broadcast(): return lax.psum(kept, axis)  434 us
    ppermute x3, waiting for transfers between devices, passed_along(): lax.ppermute(value, axis, [(i, (i + by) % peers) for i in range(peers)])  264 us
    dot_general x4, matrix products, local(): jnp.dot(received.reshape(actions * local_rows, block_width), current, pre...  40.4 us
  transfers between devices with their start and end apart: 4, of which 3 were waited for; matrix products, arithmetic and copies ran while one was open for 5% of the time, Pallas kernels for 0%

commit v1 on v0

v1 whole, which is shorter than its diff:
```python
import functools

import jax
import jax.numpy as jnp
from jax import lax
from jax.experimental import pallas as pl
from jax.experimental.pallas import tpu as pltpu
from jax.sharding import PartitionSpec as P

STEPS = 4
PIECES = 2
DISCOUNT = 0.97
MESH = pl.DeviceIdType.MESH


def kernel(
    rows, cols, t_ref, v_ref, e_ref, c_ref, out_ref,
    slots, v_buf, work, arrived, e_buf, c_buf,
    in_sem, own_sem, slot_sem, first_sem, up_sem, down_sem, sum_send, sum_recv,
):
    b = lax.axis_index("row")
    z = lax.axis_index("col")
    ratio = rows // cols
    q = b // ratio
    actions = t_ref.shape[0]
    width = v_ref.shape[0]
    half = width // PIECES
    sums = (STEPS - 1) * actions
    total = STEPS * actions

    loads = [
        pltpu.make_async_copy(v_ref, v_buf, in_sem.at[0]),
        pltpu.make_async_copy(e_ref, e_buf, in_sem.at[1]),
        pltpu.make_async_copy(c_ref, c_buf, in_sem.at[2]),
    ]
    for load in loads:
        load.start()

    barrier = pltpu.get_barrier_semaphore()
    for d in range(1, STEPS):
        for by in (d, rows - d):
            pl.semaphore_signal(barrier, inc=1, device_id=((b + by) % rows, z), device_id_type=MESH)

    @pl.when(z > 0)
    def _():
        pl.semaphore_signal(barrier, inc=1, device_id=(b, z - 1), device_id_type=MESH)

    @pl.when(z < cols - 1)
    def _():
        pl.semaphore_signal(barrier, inc=1, device_id=(b, z + 1), device_id_type=MESH)

    beside = jnp.where(z > 0, 1, 0) + jnp.where(z < cols - 1, 1, 0)
    pl.semaphore_wait(barrier, 2 * (STEPS - 1) + beside)

    def held(j, a, h):
        offset = pl.multiple_of(j * width + h * half, 128)
        return t_ref.at[a, :, pl.ds(offset, half)]

    def first_copy(j, d, a, h):
        i = (d - 1) * actions + a
        return pltpu.make_async_remote_copy(
            src_ref=held(j, a, h), dst_ref=slots.at[i, h],
            send_sem=first_sem.at[j, a, h], recv_sem=slot_sem.at[i, h],
            device_id=(z * ratio + j, z), device_id_type=MESH,
        )

    def own_copy(j, a, h):
        i = (STEPS - 1) * actions + a
        return pltpu.make_async_copy(held(j, a, h), slots.at[i, h], own_sem.at[a, h])

    def for_blocks(away, own):
        for j in range(ratio):
            d = (z * ratio + j - b + rows) % rows

            @pl.when((d > 0) & (d < STEPS))
            def _():
                @pl.loop(0, actions)
                def _(a):
                    for h in range(PIECES):
                        away(j, d, a, h)

            if own is not None:
                @pl.when(d == 0)
                def _():
                    @pl.loop(0, actions)
                    def _(a):
                        for h in range(PIECES):
                            own(j, a, h)

    for_blocks(
        lambda j, d, a, h: first_copy(j, d, a, h).start(),
        lambda j, a, h: own_copy(j, a, h).start(),
    )

    def along(i, h, by, sem):
        return pltpu.make_async_remote_copy(
            src_ref=slots.at[i, h], dst_ref=slots.at[i, h],
            send_sem=sem.at[i, h], recv_sem=slot_sem.at[i, h],
            device_id=(b, z + by), device_id_type=MESH,
        )

    goes_up = (z >= q) & (z < cols - 1)
    goes_down = (z <= q) & (z > 0)

    def sum_copy(i):
        d = i // actions + 1
        return pltpu.make_async_remote_copy(
            src_ref=work.at[i], dst_ref=arrived.at[i],
            send_sem=sum_send.at[i], recv_sem=sum_recv.at[i],
            device_id=((b - d + rows) % rows, z), device_id_type=MESH,
        )

    loads[0].wait()

    @pl.loop(0, total)
    def _(i):
        for h in range(PIECES):
            local = (i >= sums) & (z == q)

            @pl.when(local)
            def _():
                own_copy(b % ratio, i % actions, h).wait()

            @pl.when(jnp.logical_not(local))
            def _():
                along(i, h, 0, up_sem).wait_recv()

            @pl.when(goes_up)
            def _():
                along(i, h, 1, up_sem).start()

            @pl.when(goes_down)
            def _():
                along(i, h, -1, down_sem).start()

            tile = 512

            @pl.loop(0, work.shape[2] // tile)
            def _(n):
                at = pl.ds(pl.multiple_of(n * tile, tile), tile)
                product = jnp.dot(
                    slots[i, h], v_buf[h * half:(h + 1) * half, at],
                    preferred_element_type=jnp.float32,
                )
                if h == 0:
                    work[i, :, at] = product
                else:
                    work[i, :, at] += product

        @pl.when((i >= 1) & (i <= sums))
        def _():
            sum_copy(i - 1).start()

    loads[1].wait()
    loads[2].wait()

    @pl.loop(0, sums)
    def _(i):
        sum_copy(i).wait_recv()

    @pl.loop(0, out_ref.shape[0] // 16)
    def _(k):
        at = pl.ds(pl.multiple_of(k * 16, 16), 16)
        best = None
        for a in range(actions):
            backup = e_buf[a, at, :].astype(jnp.float32) + work[sums + a, at, :]
            for d in range(STEPS - 1):
                backup = backup + arrived[d * actions + a, at, :]
            cost = c_buf[a, at, :].astype(jnp.float32) + DISCOUNT * backup
            best = cost if best is None else jnp.minimum(best, cost)
        out_ref[at, :] = best

    @pl.loop(0, sums)
    def _(i):
        sum_copy(i).wait_send()

    for_blocks(lambda j, d, a, h: first_copy(j, d, a, h).wait_send(), None)

    @pl.when(goes_up)
    def _():
        @pl.loop(0, total)
        def _(i):
            for h in range(PIECES):
                along(i, h, 1, up_sem).wait_send()

    @pl.when(goes_down)
    def _():
        @pl.loop(0, total)
        def _(i):
            for h in range(PIECES):
                along(i, h, -1, down_sem).wait_send()


def local(transitions, values, earlier_sum, section_costs):
    rows = lax.axis_size("row")
    cols = lax.axis_size("col")
    actions, height, _ = transitions.shape
    width, scenarios = values.shape
    total = STEPS * actions
    sums = (STEPS - 1) * actions
    ratio = rows // cols
    anywhere = pl.BlockSpec(memory_space=pl.ANY)
    dma = pltpu.SemaphoreType.DMA
    return pl.pallas_call(
        functools.partial(kernel, rows, cols),
        out_shape=jax.ShapeDtypeStruct((height, scenarios), jnp.float32),
        in_specs=[anywhere] * 4,
        out_specs=pl.BlockSpec(memory_space=pltpu.VMEM),
        scratch_shapes=[
            pltpu.VMEM((total, PIECES, height, width // PIECES), jnp.bfloat16),
            pltpu.VMEM((width, scenarios), jnp.bfloat16),
            pltpu.VMEM((total, height, scenarios), jnp.float32),
            pltpu.VMEM((sums, height, scenarios), jnp.float32),
            pltpu.VMEM((actions, height, scenarios), jnp.bfloat16),
            pltpu.VMEM((actions, height, scenarios), jnp.bfloat16),
            dma((3,)),
            dma((actions, PIECES)),
            dma((total, PIECES)),
            dma((ratio, actions, PIECES)),
            dma((total, PIECES)),
            dma((total, PIECES)),
            dma((sums,)),
            dma((sums,)),
        ],
        compiler_params=pltpu.CompilerParams(
            collective_id=0, has_side_effects=True, vmem_limit_bytes=66_000_000
        ),
    )(transitions, values, earlier_sum, section_costs)


def solution(mesh):
    in_specs = (
        P(None, "row", "col"),
        P("row", "col"),
        P(None, "row", "col"),
        P(None, "row", "col"),
    )
    out_specs = P("row", "col")
    return jax.shard_map(local, mesh=mesh, in_specs=in_specs, out_specs=out_specs, check_vma=False)
```

time: 770 us -> 403 us (0.52)
  waiting for transfers between devices: 697 us -> 0 us
  Pallas kernels: 0 us -> 398 us
  matrix products: 40.4 us -> 0 us
  between operations: 13.5 us -> 0.01 us
  other arithmetic: 11.5 us -> 0 us
    psum x1 -> x0, waiting for transfers between devices: 434 us -> none  [broadcast(): return lax.psum(kept, axis)]
    pallas_call x0 -> x1, Pallas kernels: none -> 398 us  [local(): pl.pallas_call(functools.partial(kernel, rows, cols), out_shape=jax.Shape...]
    ppermute x3 -> x0, waiting for transfers between devices: 264 us -> none  [passed_along(): lax.ppermute(value, axis, [(i, (i + by) % peers) for i in range(peers)])]
    dot_general x4 -> x0, matrix products: 40.4 us -> none  [local(): jnp.dot(received.reshape(actions * local_rows, block_width), current, pre...]
    select_n x1 -> x0, other arithmetic: 11.5 us -> none  [broadcast(): jnp.where(lax.axis_index(axis) == source, value, 0).astype(value.dtype)]
  transfers between devices with their start and end apart: 4 -> 0, of which waited for: 3 -> 0; matrix products, arithmetic and copies ran while one was open for 5% -> 0% of each run, Pallas kernels for 0% -> 0%
where the time goes in v1:
time: 403 us; the launch traced here: 400 us
  Pallas kernels  398 us (99%)
    pallas_call x1, Pallas kernels, local(): pl.pallas_call(functools.partial(kernel, rows, cols), out_shape=jax.Shape...  398 us

profile of v1, /device:TPU:25, one launch (start us, length us, event | category | flops | bytes accessed | tf_op | source)
XLA Modules:
  0.0 399.8 jit_solution(15517942945753815844)
XLA Ops:
  0.0 397.7 %shard_map.46 = f32[128,1536]{1,0:T(8,128)} custom-call(bf16[4,128,8192]{2,1,0:T(8,128)(2,1)} %t_ref.1, bf16[4096,1536]{1,0:T(8,128)(2,1)} %v_ref.1, bf16[4,128,1536]{2,1,0:T(8,128)(2,1)} %e_ref.1, bf16[4,128,1536]{2,1,0:T(8,128)(2,1)} %c_ref.1), custom_call_target="tpu_custom_call" | custom-call | tf_op jit(solution)/shard_map/pallas_call | solution.py:204
  397.7 2.1 copy.6

commit v2 on v1

--- a/solution.py
+++ b/solution.py
@@ -14,9 +14,10 @@
 
 
 def kernel(
-    rows, cols, t_ref, v_ref, e_ref, c_ref, out_ref,
+    rows, cols, t_ref, v_ref, e_ref, c_ref, out_ref, relay,
     slots, v_buf, work, arrived, e_buf, c_buf,
     in_sem, own_sem, slot_sem, first_sem, up_sem, down_sem, sum_send, sum_recv,
+    relay_sem, pass_sem, give_sem,
 ):
     b = lax.axis_index("row")
     z = lax.axis_index("col")
@@ -37,9 +38,8 @@
         load.start()
 
     barrier = pltpu.get_barrier_semaphore()
-    for d in range(1, STEPS):
-        for by in (d, rows - d):
-            pl.semaphore_signal(barrier, inc=1, device_id=((b + by) % rows, z), device_id_type=MESH)
+    for by in range(1, rows):
+        pl.semaphore_signal(barrier, inc=1, device_id=((b + by) % rows, z), device_id_type=MESH)
 
     @pl.when(z > 0)
     def _():
@@ -50,7 +50,7 @@
         pl.semaphore_signal(barrier, inc=1, device_id=(b, z + 1), device_id_type=MESH)
 
     beside = jnp.where(z > 0, 1, 0) + jnp.where(z < cols - 1, 1, 0)
-    pl.semaphore_wait(barrier, 2 * (STEPS - 1) + beside)
+    pl.semaphore_wait(barrier, rows - 1 + beside)
 
     def held(j, a, h):
         offset = pl.multiple_of(j * width + h * half, 128)
@@ -110,28 +110,99 @@
             device_id=((b - d + rows) % rows, z), device_id_type=MESH,
         )
 
-    loads[0].wait()
-
-    @pl.loop(0, total)
-    def _(i):
+    core = b % ratio
+    source = z == q
+    feeds_up = source & (z < cols - 1)
+    feeds_down = source & (z > 0)
+
+    def to_helper(i, h, up):
+        u = q if up else cols - 1 - q
+        row = ((cols - 1) * ratio if up else 0) + core
+        return pltpu.make_async_remote_copy(
+            src_ref=slots.at[i, h], dst_ref=relay.at[u, i // actions, h],
+            send_sem=(up_sem if up else down_sem).at[i, h],
+            recv_sem=relay_sem.at[u, i // actions, h],
+            device_id=(row, z), device_id_type=MESH,
+        )
+
+    def passed(u, p, h, up):
+        return pltpu.make_async_remote_copy(
+            src_ref=relay.at[u, p, h], dst_ref=relay.at[u, p, h],
+            send_sem=pass_sem.at[u, p, h], recv_sem=relay_sem.at[u, p, h],
+            device_id=(b, z + (1 if up else -1)), device_id_type=MESH,
+        )
+
+    def given(u, p, h, up):
+        row = (u if up else cols - 1 - u) * ratio + core
+        return pltpu.make_async_remote_copy(
+            src_ref=relay.at[u, p, h], dst_ref=slots.at[p * actions, h],
+            send_sem=give_sem.at[u, p, h], recv_sem=slot_sem.at[p * actions, h],
+            device_id=(row, z), device_id_type=MESH,
+        )
+
+    def for_relay(r, u, finish):
+        p = r // actions
+        for up in (True, False):
+            y = z if up else cols - 1 - z
+            helps = (q == (cols - 1 if up else 0)) & (u <= y) & (u < cols - 1)
+
+            @pl.when(helps)
+            def _():
+                for h in range(PIECES):
+                    if not finish:
+                        passed(u, p, h, up).wait_recv()
+
+                    @pl.when(y < cols - 1)
+                    def _():
+                        copy = passed(u, p, h, up)
+                        copy.wait_send() if finish else copy.start()
+
+                    @pl.when(y > u)
+                    def _():
+                        copy = given(u, p, h, up)
+                        copy.wait_send() if finish else copy.start()
+
+    per_step = -(-(cols - 1) // actions)
+
+    def relay_step(r, finish):
+        @pl.when((r >= 0) & (r < total))
+        def _():
+            for extra in range(per_step):
+                for_relay(r, r % actions + extra * actions, finish)
+
+    def slot_of(s):
+        first = jnp.where(source, 0, 1)
+        return s // actions * actions + (s % actions + first) % actions
+
+    def own_step(s):
+        i = slot_of(s)
+        direct = i % actions > 0
         for h in range(PIECES):
-            local = (i >= sums) & (z == q)
+            local = (i >= sums) & source
 
             @pl.when(local)
             def _():
-                own_copy(b % ratio, i % actions, h).wait()
+                own_copy(core, i % actions, h).wait()
 
             @pl.when(jnp.logical_not(local))
             def _():
                 along(i, h, 0, up_sem).wait_recv()
 
-            @pl.when(goes_up)
+            @pl.when(goes_up & direct)
             def _():
                 along(i, h, 1, up_sem).start()
 
-            @pl.when(goes_down)
+            @pl.when(goes_down & direct)
             def _():
                 along(i, h, -1, down_sem).start()
+
+            @pl.when(feeds_up & jnp.logical_not(direct))
+            def _():
+                to_helper(i, h, True).start()
+
+            @pl.when(feeds_down & jnp.logical_not(direct))
+            def _():
+                to_helper(i, h, False).start()
 
             tile = 512
 
@@ -147,9 +218,20 @@
                 else:
                     work[i, :, at] += product
 
-        @pl.when((i >= 1) & (i <= sums))
+        @pl.when((s >= 1) & (s <= sums))
         def _():
-            sum_copy(i - 1).start()
+            sum_copy(slot_of(s - 1)).start()
+
+    loads[0].wait()
+    lag = 2 * jnp.where(q == 0, cols - 1 - z, z)
+
+    @pl.loop(0, total + 2 * cols)
+    def _(t):
+        relay_step(t - lag, False)
+
+        @pl.when((t >= cols) & (t < cols + total))
+        def _():
+            own_step(t - cols)
 
     loads[1].wait()
     loads[2].wait()
@@ -176,19 +258,19 @@
 
     for_blocks(lambda j, d, a, h: first_copy(j, d, a, h).wait_send(), None)
 
-    @pl.when(goes_up)
-    def _():
-        @pl.loop(0, total)
-        def _(i):
-            for h in range(PIECES):
+    @pl.loop(0, total)
+    def _(i):
+        direct = i % actions > 0
+        for h in range(PIECES):
+            @pl.when((goes_up & direct) | (feeds_up & jnp.logical_not(direct)))
+            def _():
                 along(i, h, 1, up_sem).wait_send()
 
-    @pl.when(goes_down)
-    def _():
-        @pl.loop(0, total)
-        def _(i):
-            for h in range(PIECES):
+            @pl.when((goes_down & direct) | (feeds_down & jnp.logical_not(direct)))
+            def _():
                 along(i, h, -1, down_sem).wait_send()
+
+        relay_step(i, True)
 
 
 def local(transitions, values, earlier_sum, section_costs):
@@ -203,9 +285,14 @@
     dma = pltpu.SemaphoreType.DMA
     return pl.pallas_call(
         functools.partial(kernel, rows, cols),
-        out_shape=jax.ShapeDtypeStruct((height, scenarios), jnp.float32),
+        out_shape=(
+            jax.ShapeDtypeStruct((height, scenarios), jnp.float32),
+            jax.ShapeDtypeStruct(
+                (cols - 1, STEPS, PIECES, height, width // PIECES), jnp.bfloat16
+            ),
+        ),
         in_specs=[anywhere] * 4,
-        out_specs=pl.BlockSpec(memory_space=pltpu.VMEM),
+        out_specs=(pl.BlockSpec(memory_space=pltpu.VMEM), anywhere),
         scratch_shapes=[
             pltpu.VMEM((total, PIECES, height, width // PIECES), jnp.bfloat16),
             pltpu.VMEM((width, scenarios), jnp.bfloat16),
@@ -221,11 +308,14 @@
             dma((total, PIECES)),
             dma((sums,)),
             dma((sums,)),
+            dma((cols - 1, STEPS, PIECES)),
+            dma((cols - 1, STEPS, PIECES)),
+            dma((cols - 1, STEPS, PIECES)),
         ],
         compiler_params=pltpu.CompilerParams(
             collective_id=0, has_side_effects=True, vmem_limit_bytes=66_000_000
         ),
-    )(transitions, values, earlier_sum, section_costs)
+    )(transitions, values, earlier_sum, section_costs)[0]
 
 
 def solution(mesh):

time: 403 us -> 554 us (1.37)
  Pallas kernels: 398 us -> 552 us
    pallas_call x1, Pallas kernels: 398 us -> 552 us  [local(): pl.pallas_call(functools.partial(kernel, rows, cols), out_shape=(jax.Shap...]
where the time goes in v2:
time: 554 us
  Pallas kernels  552 us (100%)
    pallas_call x1, Pallas kernels, local(): pl.pallas_call(functools.partial(kernel, rows, cols), out_shape=(jax.Shap...  552 us

profile of v2, /device:TPU:25, one launch (start us, length us, event | category | flops | bytes accessed | tf_op | source)
XLA Modules:
  0.0 553.9 jit_solution(4866624262279183303)
XLA Ops:
  0.0 551.8 %shard_map.46 = (f32[128,1536]{1,0:T(8,128)}, bf16[3,4,2,128,2048]{4,3,2,1,0:T(8,128)(2,1)}) custom-call(bf16[4,128,8192]{2,1,0:T(8,128)(2,1)} %t_ref.1, bf16[4096,1536]{1,0:T(8,128)(2,1)} %v_ref.1, bf16[4,128,1536]{2,1,0:T(8,128)(2,1)} %e_ref.1, bf16[4,128,1536]{2,1,0:T(8,128)(2,1)} %c_ref.1), custom_call_target="tpu_custom_call" | custom-call | tf_op jit(solution)/shard_map/pallas_call | solution.py:286
  551.8 2.1 copy.6

commit v3 on v1

--- a/solution.py
+++ b/solution.py
@@ -8,7 +8,7 @@
 from jax.sharding import PartitionSpec as P
 
 STEPS = 4
-PIECES = 2
+PIECES = 4
 DISCOUNT = 0.97
 MESH = pl.DeviceIdType.MESH
 
@@ -110,7 +110,25 @@
             device_id=((b - d + rows) % rows, z), device_id_type=MESH,
         )
 
-    loads[0].wait()
+    def finish(a):
+        for d in range(STEPS - 1):
+            sum_copy(d * actions + a).wait_recv()
+
+        @pl.loop(0, out_ref.shape[0] // 16)
+        def _(k):
+            at = pl.ds(pl.multiple_of(k * 16, 16), 16)
+            backup = e_buf[a, at, :].astype(jnp.float32) + work[sums + a, at, :]
+            for d in range(STEPS - 1):
+                backup = backup + arrived[d * actions + a, at, :]
+            cost = c_buf[a, at, :].astype(jnp.float32) + DISCOUNT * backup
+
+            @pl.when(a == 0)
+            def _():
+                out_ref[at, :] = cost
+
+            @pl.when(a > 0)
+            def _():
+                out_ref[at, :] = jnp.minimum(out_ref[at, :], cost)
 
     @pl.loop(0, total)
     def _(i):
@@ -132,6 +150,12 @@
             @pl.when(goes_down)
             def _():
                 along(i, h, -1, down_sem).start()
+
+            if h == 0:
+                @pl.when(i == 0)
+                def _():
+                    for load in loads:
+                        load.wait()
 
             tile = 512
 
@@ -151,24 +175,11 @@
         def _():
             sum_copy(i - 1).start()
 
-    loads[1].wait()
-    loads[2].wait()
-
-    @pl.loop(0, sums)
-    def _(i):
-        sum_copy(i).wait_recv()
-
-    @pl.loop(0, out_ref.shape[0] // 16)
-    def _(k):
-        at = pl.ds(pl.multiple_of(k * 16, 16), 16)
-        best = None
-        for a in range(actions):
-            backup = e_buf[a, at, :].astype(jnp.float32) + work[sums + a, at, :]
-            for d in range(STEPS - 1):
-                backup = backup + arrived[d * actions + a, at, :]
-            cost = c_buf[a, at, :].astype(jnp.float32) + DISCOUNT * backup
-            best = cost if best is None else jnp.minimum(best, cost)
-        out_ref[at, :] = best
+        @pl.when(i > sums)
+        def _():
+            finish(i - 1 - sums)
+
+    finish(actions - 1)
 
     @pl.loop(0, sums)
     def _(i):

time: 403 us -> 391 us (0.970)
  Pallas kernels: 398 us -> 385 us
    pallas_call x1, Pallas kernels: 398 us -> 385 us  [local(): pl.pallas_call(functools.partial(kernel, rows, cols), out_shape=jax.Shape...]
where the time goes in v3:
time: 391 us; the launch traced here: 387 us
  Pallas kernels  385 us (98%)
    pallas_call x1, Pallas kernels, local(): pl.pallas_call(functools.partial(kernel, rows, cols), out_shape=jax.Shape...  385 us

profile of v3, /device:TPU:25, one launch (start us, length us, event | category | flops | bytes accessed | tf_op | source)
XLA Modules:
  0.0 387.1 jit_solution(4758208837742995428)
XLA Ops:
  0.0 385.0 %shard_map.46 = f32[128,1536]{1,0:T(8,128)} custom-call(bf16[4,128,8192]{2,1,0:T(8,128)(2,1)} %t_ref.1, bf16[4096,1536]{1,0:T(8,128)(2,1)} %v_ref.1, bf16[4,128,1536]{2,1,0:T(8,128)(2,1)} %e_ref.1, bf16[4,128,1536]{2,1,0:T(8,128)(2,1)} %c_ref.1), custom_call_target="tpu_custom_call" | custom-call | tf_op jit(solution)/shard_map/pallas_call | solution.py:215
  385.0 2.1 copy.6

commit v4 on v3

--- a/solution.py
+++ b/solution.py
@@ -8,7 +8,7 @@
 from jax.sharding import PartitionSpec as P
 
 STEPS = 4
-PIECES = 4
+PIECES = 8
 DISCOUNT = 0.97
 MESH = pl.DeviceIdType.MESH
 

time: 391 us -> 387 us (0.990)
  no operation moved by 1% of the time
where the time goes in v4:
time: 387 us; the launch traced here: 384 us
  Pallas kernels  382 us (99%)
    pallas_call x1, Pallas kernels, local(): pl.pallas_call(functools.partial(kernel, rows, cols), out_shape=jax.Shape...  382 us

profile of v4, /device:TPU:25, one launch (start us, length us, event | category | flops | bytes accessed | tf_op | source)
XLA Modules:
  0.0 383.8 jit_solution(6278067418965065267)
XLA Ops:
  0.0 381.7 %shard_map.46 = f32[128,1536]{1,0:T(8,128)} custom-call(bf16[4,128,8192]{2,1,0:T(8,128)(2,1)} %t_ref.1, bf16[4096,1536]{1,0:T(8,128)(2,1)} %v_ref.1, bf16[4,128,1536]{2,1,0:T(8,128)(2,1)} %e_ref.1, bf16[4,128,1536]{2,1,0:T(8,128)(2,1)} %c_ref.1), custom_call_target="tpu_custom_call" | custom-call | tf_op jit(solution)/shard_map/pallas_call | solution.py:215
  381.7 2.1 copy.6
